TPU v7x, 32 devices: a whole 2x2x4 slice. The times are simulated.
32 devices in a mesh: groups: 2 (over y), section: 2 (over core), row: 2 (over x), col: 4 (over z).
Axes of the slice: x: 2, y: 2, z: 4, core: 2. Of those that a mesh axis runs over, the one named last changes fastest.
Arguments:
- mid: bfloat16 [2, 768, 8192], P('section', ('groups', 'col'), 'row'), parts along dimension 1, may hold values from -12000 to 12000
- query_grad: bfloat16 [2, 768, 8192], P('section', ('groups', 'row'), 'col'), parts along dimension 1, may hold values from -6 to 6
- top_grad: bfloat16 [768, 8192], P(('groups', 'col'), 'row'), parts along dimension 0, may hold values from -6 to 6
- w_query: bfloat16 [2, 8192, 8192], P('section', 'row', 'col'), may hold values from -0.0625 to 0.0625
- gain: float32 [2, 8192], P('section', 'row'), may hold values from 0.5 to 1.5
Outputs:
- weight_grad: bfloat16 [4, 8192, 8192], P(('groups', 'section'), 'row', 'col'), parts along dimension 0
- residual_grad: bfloat16 [2, 768, 8192], P('section', ('groups', 'col'), 'row'), parts along dimension 1
There are 2 independent parts, one for each index of `groups`. A program takes and returns all parts, laid end to end along the dimension named above; an argument that names none is the same for every part. Nothing has to cross between parts.
All inputs are finite; a program needn't handle non-finite values.
Results may differ from a plain program's by a relative error of at most 0.0085.
Values may be sent and summed in bfloat16 or wider, within the bound.
A program may use at most 128 MiB of HBM per device.

v0:
```python
import jax
import jax.numpy as jnp
from jax import lax
from jax.sharding import PartitionSpec as P

EPSILON = 1e-05


def carried_in(x, axis, combine, identity):
    peers, mine = (lax.axis_size(axis), lax.axis_index(axis))
    everything = lax.all_gather(x.astype(jnp.bfloat16), axis)
    start = jnp.broadcast_to(jnp.asarray(identity, x.dtype), x.shape)

    def lap(k, before):
        at = peers - 1 - k
        reached = at > mine
        new = combine(before, everything[at].astype(x.dtype))
        return jnp.where(reached, new, before)

    return lax.fori_loop(0, peers, lap, start)


def body(mid, query_grad, top_grad, w_query, gain):
    x_rows = mid[0]
    x_float = x_rows.astype(jnp.float32)
    gains = gain[0]
    weights = w_query[0]
    width = weights.shape[0] * lax.axis_size("row")
    local_rows = x_rows.shape[0]
    total_rows = local_rows * lax.axis_size("col")
    grads_all = lax.all_gather(query_grad[0], "row", axis=0, tiled=True)
    block = grads_all
    normed_grad = lax.psum_scatter(
        lax.dot_general(
            block, weights, (((1,), (1,)), ((), ())), preferred_element_type=jnp.float32
        ).astype(jnp.bfloat16),
        "col",
        scatter_dimension=0,
        tiled=True,
    ).astype(jnp.float32)
    products = jnp.sum(x_float * gains * normed_grad, axis=1)
    squares, products = lax.psum((jnp.sum(x_float * x_float, axis=1), products), "row")
    inverse = lax.rsqrt(squares / width + EPSILON)
    normed = (x_float * inverse[:, None] * gains).astype(jnp.bfloat16)
    block = grads_all
    contracted = lax.dot_general(
        lax.all_gather(normed, "col", axis=0, tiled=True),
        block,
        (((0,), (0,)), ((), ())),
        preferred_element_type=jnp.float32,
    )
    weight_grad = (contracted * total_rows ** (-0.5)).astype(jnp.bfloat16)[None]
    own_term = (
        inverse[:, None] * gains * normed_grad - x_float * (inverse**3 * products / width)[:, None]
    )
    later = carried_in(
        own_term, "section", lambda earlier, latest: earlier + latest, jnp.zeros_like(own_term)
    )
    residual = (top_grad.astype(jnp.float32) + later + own_term).astype(jnp.bfloat16)[None]
    return (weight_grad, residual)


def solution(mesh):
    return jax.shard_map(
        body,
        mesh=mesh,
        in_specs=(
            P("section", ("groups", "col"), "row"),
            P("section", ("groups", "row"), "col"),
            P(("groups", "col"), "row"),
            P("section", "row", "col"),
            P("section", "row"),
        ),
        out_specs=(P(("groups", "section"), "row", "col"), P("section", ("groups", "col"), "row")),
        check_vma=False,
    )
```

profile of v0, /device:TPU:0, one launch (start us, length us, event | category | flops | bytes accessed | tf_op | source)
XLA Modules:
  0.0 222.5 jit_solution(8023392890706824762)
XLA Ops:
  7.2 0.0 all-gather.8.cloned.1.call-start
  7.2 0.7 all-gather.8.cloned.1.call-update
  7.9 0.0 reduce-scatter.2.cloned.1.call-start
  7.9 31.5 %all-gather.8.cloned.1.call-done = bf16[1,384,2048]{2,1,0:T(8,128)(2,1)} async-done(((bf16[1,192,2048]{2,1,0:T(8,128)(2,1)}), bf16[1,384,2048]{2,1,0:T(8,128)(2,1)}) %all-gather.8.cloned.1.call-update) | async-done | bytes 1572880 | tf_op jit(solution)/shard_map/all_gather | solution.py:31
  39.5 11.8 %fusion.3 = bf16[384,4096]{1,0:T(8,128)(2,1)} fusion(bf16[1,4096,2048]{2,1,0:T(8,128)(2,1)} %param.10, bf16[1,384,2048]{2,1,0:T(8,128)(2,1)} %all-gather.8.cloned.1.call-done), kind=kOutput, calls=%fused_computation.5 | convolution fusion | flops 6444023808 | bytes 21495808 | tf_op jit(solution)/shard_map/dot_general | solution.py:34
  51.3 0.0 reduce-scatter.2.cloned.1.call-update
  51.3 0.0 all-gather.10.cloned.1.call-start
  51.4 60.4 %reduce-scatter.2.cloned.1.call-done = bf16[96,4096]{1,0:T(8,128)(2,1)} async-done(((bf16[384,4096]{1,0:T(8,128)(2,1)}), bf16[96,4096]{1,0:T(8,128)(2,1)}) %reduce-scatter.2.cloned.1.call-update) | async-done | bytes 786448 | tf_op jit(solution)/shard_map/reduce_scatter | solution.py:33
  111.8 0.0 copy-done
  111.8 0.0 copy-done.2
  111.8 1.7 fusion.7
  113.4 4.9 %all-reduce = (f32[96]{0:T(128)S(1)}, f32[96]{0:T(128)S(1)}) all-reduce(f32[96]{0:T(128)S(1)} %get-tuple-element.129, f32[96]{0:T(128)S(1)} %get-tuple-element.128), channel_id=1, replica_groups=mesh['groups'=2,'section'=2,'row'=2,'col'=4] {'row'}, use_global_device_ids=true, to_apply=%region_1.0 | all-reduce | flops 192 | bytes 1536 | tf_op jit(solution)/shard_map/psum | solution.py:42
  118.4 0.0 copy-done.1
  118.4 1.3 fusion.13
  119.7 0.0 all-gather.10.cloned.1.call-update
  119.7 0.0 all-gather.6.cloned.1.call-start
  119.8 9.9 %all-gather.10.cloned.1.call-done = bf16[192,4096]{1,0:T(8,128)(2,1)} async-done(((bf16[96,4096]{1,0:T(8,128)(2,1)}), bf16[192,4096]{1,0:T(8,128)(2,1)}) %all-gather.10.cloned.1.call-update) | async-done | bytes 1572880 | tf_op jit(solution)/shard_map/all_gather | solution.py:11
  129.7 4.0 %while.16 = (s32[]{:T(128)}, f32[96,4096]{1,0:T(8,128)S(1)}, s32[]{:T(128)}, bf16[2,96,4096]{2,1,0:T(8,128)(2,1)}, s32[]{:T(128)}, /*index=5*/s32[]{:T(128)}, s32[]{:T(128)}) while((s32[]{:T(128)}, f32[96,4096]{1,0:T(8,128)S(1)}, s32[]{:T(128)}, bf16[2,96,4096]{2,1,0:T(8,128)(2,1)}, s32[]{:T(128)}, /*index=5*/s32[]{:T(128)}, ...), condition=%wide.region_6.7_spmd.clone, body=%wide.region_5.6_spmd.clone.sunk | while | flops 1572872 | bytes 3932315 | solution.py:20
  129.7 2.0 add_select_fusion.2
  131.7 2.0 add_select_fusion.2
  133.7 3.0 %fusion.14 = (bf16[1,96,4096]{2,1,0:T(8,128)(2,1)}, bf16[96,4096]{1,0:T(8,128)(2,1)}) fusion(bf16[96,4096]{1,0:T(8,128)(2,1)S(1)} %copy-done.1, f32[96,4096]{1,0:T(8,128)S(1)} %get-tuple-element.112, bf16[96,4096]{1,0:T(8,128)(2,1)} %param.9, bf16[1,96,4096]{2,1,0:T(8,128)(2,1)S(1)} %copy-done, f32[96]{0:T(128)S(1)} %get-tuple-element.142, ...), kind=kLoop, calls=%fused_computation.21 | loop fusion | flops 5111808 | bytes 5522176 | tf_op jit(solution)/shard_map/broadcast_in_dim | solution.py:59
  136.7 0.0 all-gather.6.cloned.1.call-update
  136.7 64.8 %all-gather.6.cloned.1.call-done = bf16[384,4096]{1,0:T(8,128)(2,1)} async-done(((bf16[96,4096]{1,0:T(8,128)(2,1)}), bf16[384,4096]{1,0:T(8,128)(2,1)}) %all-gather.6.cloned.1.call-update) | async-done | bytes 3145744 | tf_op jit(solution)/shard_map/all_gather | solution.py:47
  201.6 14.4 %fusion = bf16[1,4096,2048]{2,1,0:T(8,128)(2,1)} fusion(bf16[384,4096]{1,0:T(8,128)(2,1)} %all-gather.6.cloned.1.call-done, bf16[1,384,2048]{2,1,0:T(8,128)(2,1)} %all-gather.8.cloned.1.call-done), kind=kOutput, calls=%fused_computation.2 | convolution fusion | flops 6459228160 | bytes 21495808 | tf_op jit(solution)/shard_map/dot_general | solution.py:46
  (5 shorter events, 0.0 us)
Async XLA Ops:
  7.2 32.3 %all-gather.8.cloned.1.call-start = ((), (), s32[]{:S(2)}) async-start(), calls=%async_computation.3 | async-start | bytes 2359296 | tf_op jit(solution)/shard_map/all_gather | solution.py:31
  7.9 103.9 %reduce-scatter.2.cloned.1.call-start = ((), (), s32[]{:S(2)}) async-start(), calls=%async_computation.2 | async-start | bytes 3932160 | tf_op jit(solution)/shard_map/reduce_scatter | solution.py:33
  51.3 60.4 %copy-start = (bf16[1,96,4096]{2,1,0:T(8,128)(2,1)S(1)}, bf16[1,96,4096]{2,1,0:T(8,128)(2,1)}, u32[]{:S(2)}) copy-start(bf16[1,96,4096]{2,1,0:T(8,128)(2,1)} %param.7) | copy-start | bytes 2359300
  51.3 60.4 %copy-start.2 = (f32[1,4096]{1,0:T(1,128)S(1)}, f32[1,4096]{1,0:T(1,128)}, u32[]{:S(2)}) copy-start(f32[1,4096]{1,0:T(1,128)} %param.11) | copy-start | bytes 49156
  51.3 78.4 %all-gather.10.cloned.1.call-start = ((), (), s32[]{:S(2)}) async-start(), calls=%async_computation.4 | async-start | bytes 2359296 | tf_op jit(solution)/shard_map/all_gather | solution.py:11
  111.8 6.6 %copy-start.1 = (bf16[96,4096]{1,0:T(8,128)(2,1)S(1)}, bf16[96,4096]{1,0:T(8,128)(2,1)}, u32[]{:S(2)}) copy-start(bf16[96,4096]{1,0:T(8,128)(2,1)} %reduce-scatter.2.cloned.1.call-done) | copy-start | bytes 2359300
  119.7 81.9 %all-gather.6.cloned.1.call-start = ((), (), s32[]{:S(2)}) async-start(), calls=%async_computation.1 | async-start | bytes 3932160 | tf_op jit(solution)/shard_map/all_gather | solution.py:47
Sparse Core Ops, SparseCore 0:
  9.5 29.8 all-gather.7
  51.5 60.2 reduce-scatter.1
  119.8 9.8 all-gather.9
  136.9 64.6 all-gather.5
where the time goes:
time: 223 us
  waiting for transfers between devices  167 us (75%)
  matrix products  26.3 us (12%)
  between operations  13.8 us (6%)
  other arithmetic  9.93 us (4%)
  blocking collectives  4.94 us (2%)
    all_gather x1, waiting for transfers between devices, body(): lax.all_gather(normed, 'col', axis=0, tiled=True)  64.8 us
    reduce_scatter x1, waiting for transfers between devices, body(): lax.psum_scatter(lax.dot_general(block, weights, (((1,), (1,)), ((), ()))...  60.4 us
    all_gather x1, waiting for transfers between devices, body(): grads_all = lax.all_gather(query_grad[0], 'row', axis=0, tiled=True)  31.5 us
    dot_general x1, matrix products, body(): lax.dot_general(lax.all_gather(normed, 'col', axis=0, tiled=True), block,...  14.4 us
    dot_general x1, matrix products, body(): lax.dot_general(block, weights, (((1,), (1,)), ((), ())), preferred_eleme...  11.8 us
    all_gather x1, waiting for transfers between devices, carried_in(): everything = lax.all_gather(x.astype(jnp.bfloat16), axis)  9.93 us
    psum x1, blocking collectives, body(): lax.psum((jnp.sum(x_float * x_float, axis=1), products), 'row')  4.94 us
  transfers between devices with their start and end apart: 4, of which 4 were waited for; matrix products, arithmetic and copies ran while one was open for 0% of the time, Pallas kernels for 0%

commit v1 on v0

v1 whole, which is shorter than its diff:
```python
import functools

import jax
import jax.numpy as jnp
from jax import lax
from jax.experimental import pallas as pl
from jax.experimental.pallas import tpu as pltpu
from jax.sharding import PartitionSpec as P

EPSILON = 1e-05
LANES = 128
ROWS = 16
F32 = jnp.float32
BF16 = jnp.bfloat16


def lane_sums(value):
    total = value[:, :LANES]
    for at in range(LANES, value.shape[1], LANES):
        total = total + value[:, at : at + LANES]
    return total


def push(src, dst, send, recv, axis, peer):
    return pltpu.make_async_remote_copy(
        src_ref=src,
        dst_ref=dst,
        send_sem=send,
        recv_sem=recv,
        device_id={axis: peer},
        device_id_type=pl.DeviceIdType.MESH,
    )


def kernel(
    n_sec, n_row, n_col, chunks, halves, parts,
    mid, query, top, gain, w_hbm,
    res, normed_hbm, query_hbm,
    w_v, mid_all, query_all, part, from_left, from_right,
    squares, squares_in, prods, prods_in, grad, term, later, total, normed, scales,
    w_sem, x_right, x_left, x_recv, ag_right, ag_left, ag_recv,
    rs_right, rs_left, rs_from_left, rs_from_right,
    sq_send, sq_recv, pr_send, pr_recv, term_send, term_recv, out_sem,
):
    me_s, me_r, me_c = (lax.axis_index(a) for a in ("section", "row", "col"))
    tokens, width = mid.shape
    subs = query.shape[0]
    fc = width // chunks
    tile = min(512, fc)
    full = width * n_row
    has_left, has_right = me_c > 0, me_c < n_col - 1

    def w_copy(ch):
        rows = pl.ds(pl.multiple_of(ch * fc, fc), fc)
        return pltpu.make_async_copy(w_hbm.at[rows], w_v.at[rows], w_sem.at[ch])

    for ch in range(chunks):
        w_copy(ch).start()

    barrier = pltpu.get_barrier_semaphore()

    def greet(axis, peer):
        pl.semaphore_signal(
            barrier, inc=1, device_id={axis: peer}, device_id_type=pl.DeviceIdType.MESH
        )

    for k in range(1, n_row):
        greet("row", lax.rem(me_r + k, n_row))
    for k in range(1, n_sec):
        greet("section", lax.rem(me_s + k, n_sec))
    pl.when(has_left)(lambda: greet("col", me_c - 1))
    pl.when(has_right)(lambda: greet("col", me_c + 1))
    beside = (me_c + n_col - 1) // n_col + (2 * n_col - 2 - me_c) // n_col
    pl.semaphore_wait(barrier, n_row - 1 + n_sec - 1 + beside)

    def x_send(k, sub, right):
        piece = me_r - k if right else me_r + k
        shard = piece * subs + sub
        src = query.at[sub] if k == 0 else query_all.at[shard]
        return push(
            src, query_all.at[shard], (x_right if right else x_left).at[shard], x_recv.at[shard],
            "row", me_r + 1 if right else me_r - 1,
        )

    def x_sends(k, right):
        if right:
            return (me_r - k >= 0) & (me_r < n_row - 1)
        return (me_r + k < n_row) & (me_r > 0)

    def order(right):
        return range(subs) if right else range(subs - 1, -1, -1)

    for right in (True, False):
        @pl.when(x_sends(0, right))
        def _():
            for sub in order(right):
                x_send(0, sub, right).start()

    half = tokens // halves

    def ag_send(k, h, right):
        shard = me_c - k if right else me_c + k
        rows = pl.ds(h * half, half)
        src = mid.at[rows] if k == 0 else mid_all.at[shard, rows]
        return push(
            src, mid_all.at[shard, rows], (ag_right if right else ag_left).at[shard, h],
            ag_recv.at[shard, h], "col", me_c + 1 if right else me_c - 1,
        )

    def ag_sends(k, right):
        if right:
            return (me_c - k >= 0) & has_right
        return (me_c + k < n_col) & has_left

    for h in range(halves):
        for right in (True, False):
            pl.when(ag_sends(0, right))(lambda: ag_send(0, h, right).start())

    def ag_step(k):
        for h in range(halves):
            for right in (True, False):
                shard = me_c - k if right else me_c + k

                @pl.when((shard >= 0) if right else (shard < n_col))
                def _():
                    rows = pl.ds(h * half, half)
                    got = mid_all.at[shard, rows]
                    pltpu.make_async_copy(got, got, ag_recv.at[shard, h]).wait()
                    if k < n_col - 1:
                        pl.when(ag_sends(k, right))(lambda: ag_send(k, h, right).start())

    def product(shard, count, load, first):
        def lap(ch, _):
            if first:
                w_copy(ch).wait()
            for t in range(fc // tile):
                rows = pl.ds(pl.multiple_of(ch * fc + t * tile, tile), tile)
                value = lax.dot_general(
                    load(), w_v[rows, :], (((1,), (1,)), ((), ())), preferred_element_type=F32
                ).astype(BF16)
                for at in range(count):
                    part[shard + at, ch, :, t * tile : (t + 1) * tile] = value[
                        at * tokens : (at + 1) * tokens
                    ]
            return 0

        lax.fori_loop(0, chunks, lap, 0)

    mid_all[me_c] = mid[...]
    for sub in range(subs):
        query_all[me_r * subs + sub] = query[sub]
    product(me_r * subs, subs, lambda: query[...].reshape(subs * tokens, query.shape[2]), True)

    @pl.when(jnp.logical_not(has_left))
    def _():
        from_left[0] = jnp.zeros(from_left.shape[1:], BF16)

    @pl.when(jnp.logical_not(has_right))
    def _():
        from_right[n_col - 1] = jnp.zeros(from_right.shape[1:], BF16)

    def x_step(k, at):
        for right in (True, False):
            piece = me_r - k if right else me_r + k
            sub = at if right else subs - 1 - at
            shard = piece * subs + sub

            @pl.when((piece >= 0) if right else (piece < n_row))
            def _():
                got = query_all.at[shard]
                pltpu.make_async_copy(got, got, x_recv.at[shard]).wait()
                if k < n_row - 1:
                    pl.when(x_sends(k, right))(lambda: x_send(k, sub, right).start())
                product(shard, 1, lambda: query_all[shard], False)

    def rs_send(shard, ch, right):
        return push(
            part.at[shard, ch], (from_left if right else from_right).at[shard, ch],
            (rs_right if right else rs_left).at[shard, ch],
            (rs_from_left if right else rs_from_right).at[shard, ch],
            "col", me_c + 1 if right else me_c - 1,
        )

    def rs_shard(step, right):
        if right:
            shard = n_col - 1 - (step - me_c)
            return shard, (step >= me_c) & (shard > me_c)
        shard = step - (n_col - 1 - me_c)
        return shard, (shard >= 0) & (shard < me_c)

    def rs_wait(shard, ch, right):
        got = (from_left if right else from_right).at[shard, ch]
        pltpu.make_async_copy(
            got, got, (rs_from_left if right else rs_from_right).at[shard, ch]
        ).wait()

    def rs_step(step):
        for ch in range(chunks):
            for right in (True, False):
                shard, valid = rs_shard(step, right)

                @pl.when(valid)
                def _():
                    @pl.when(has_left if right else has_right)
                    def _():
                        rs_wait(shard, ch, right)
                        came = from_left if right else from_right

                        def lap(i, _):
                            rows = pl.ds(pl.multiple_of(i * ROWS, ROWS), ROWS)
                            part[shard, ch, rows, :] = (
                                part[shard, ch, rows, :].astype(F32)
                                + came[shard, ch, rows, :].astype(F32)
                            ).astype(BF16)
                            return 0

                        lax.fori_loop(0, tokens // ROWS, lap, 0)

                    rs_send(shard, ch, right).start()

    steps = [(k, at) for k in range(1, n_row) for at in range(subs)]
    for k, at in steps[:-1]:
        x_step(k, at)
    if subs > 1:
        rs_step(0)
    if n_col > 1:
        ag_step(1)
    for k, at in steps[-1:]:
        x_step(k, at)
    if subs == 1:
        rs_step(0)
    query_out = pltpu.make_async_copy(query_all, query_hbm, out_sem.at[0])
    query_out.start()
    for step in range(1, n_col - 1):
        ag_step(step + 1)
        if step == n_col - 2:
            break
        rs_step(step)

    def square_lap(i, _):
        shard, at = i // (tokens // ROWS), i % (tokens // ROWS)
        rows = pl.ds(pl.multiple_of(at * ROWS, ROWS), ROWS)
        value = mid_all[shard, rows, :].astype(F32)
        squares[shard, rows, :] = lane_sums(value * value)
        return 0

    lax.fori_loop(0, n_col * (tokens // ROWS), square_lap, 0)

    def sq_copy(k):
        return push(
            squares, squares_in.at[me_r], sq_send.at[k], sq_recv.at[me_r],
            "row", lax.rem(me_r + k, n_row),
        )

    def pr_copy(k):
        return push(
            prods, prods_in.at[me_r], pr_send.at[k], pr_recv.at[me_r],
            "row", lax.rem(me_r + k, n_row),
        )

    def await_from(ref, sem):
        for k in range(1, n_row):
            peer = lax.rem(me_r + k, n_row)
            got = ref.at[peer]
            pltpu.make_async_copy(got, got, sem.at[peer]).wait()

    for k in range(1, n_row):
        sq_copy(k).start()
    if n_col > 2:
        rs_step(n_col - 2)
    await_from(squares_in, sq_recv)

    def normed_lap(i, _):
        shard, at = i // (tokens // ROWS), i % (tokens // ROWS)
        rows = pl.ds(pl.multiple_of(at * ROWS, ROWS), ROWS)
        summed = squares[shard, rows, :]
        for k in range(1, n_row):
            summed = summed + squares_in[lax.rem(me_r + k, n_row), shard, rows, :]
        inverse = lax.rsqrt(jnp.sum(summed, axis=1, keepdims=True) / full + EPSILON)
        scales[shard, rows, :] = jnp.broadcast_to(inverse, (ROWS, LANES))
        value = mid_all[shard, rows, :].astype(F32)
        normed[shard, rows, :] = (value * inverse * gain[...]).astype(BF16)
        return 0

    lax.fori_loop(0, n_col * (tokens // ROWS), normed_lap, 0)
    normed_out = pltpu.make_async_copy(normed, normed_hbm, out_sem.at[1])
    normed_out.start()

    prods[...] = jnp.zeros(prods.shape, F32)
    for ch in range(chunks):
        pl.when(has_left)(lambda: rs_wait(me_c, ch, True))
        pl.when(has_right)(lambda: rs_wait(me_c, ch, False))
        cols = slice(ch * fc, (ch + 1) * fc)

        def grad_lap(i, _):
            rows = pl.ds(pl.multiple_of(i * ROWS, ROWS), ROWS)
            value = (
                part[me_c, ch, rows, :].astype(F32)
                + from_left[me_c, ch, rows, :].astype(F32)
                + from_right[me_c, ch, rows, :].astype(F32)
            ) * gain[:, cols]
            grad[rows, cols] = value
            prods[rows, :] += lane_sums(mid[rows, cols].astype(F32) * value)
            return 0

        lax.fori_loop(0, tokens // ROWS, grad_lap, 0)
    for k in range(1, n_row):
        pr_copy(k).start()
    await_from(prods_in, pr_recv)

    piece = tokens // parts

    def term_copy(to, at):
        rows = pl.ds(at * piece, piece)
        return push(
            term.at[rows], later.at[me_s, rows], term_send.at[to, at], term_recv.at[me_s, at],
            "section", to,
        )

    for at in range(parts):
        def term_lap(i, _):
            rows = pl.ds(pl.multiple_of(at * piece + i * ROWS, ROWS), ROWS)
            summed = prods[rows, :]
            for k in range(1, n_row):
                summed = summed + prods_in[lax.rem(me_r + k, n_row), rows, :]
            inverse = scales[me_c, rows, :][:, :1]
            scale = inverse**3 * jnp.sum(summed, axis=1, keepdims=True) / full
            own = inverse * grad[rows, :] - mid[rows, :].astype(F32) * scale
            term[rows, :] = own.astype(BF16)
            total[rows, :] = top[rows, :].astype(F32) + own
            return 0

        lax.fori_loop(0, piece // ROWS, term_lap, 0)
        for to in range(n_sec - 1):
            pl.when(me_s > to)(lambda: term_copy(to, at).start())
    for at in range(parts):
        for source in range(1, n_sec):
            @pl.when(me_s < source)
            def _():
                span = pl.ds(at * piece, piece)
                got = later.at[source, span]
                pltpu.make_async_copy(got, got, term_recv.at[source, at]).wait()

                def later_lap(i, _):
                    rows = pl.ds(pl.multiple_of(at * piece + i * ROWS, ROWS), ROWS)
                    total[rows, :] += later[source, rows, :].astype(F32)
                    return 0

                lax.fori_loop(0, piece // ROWS, later_lap, 0)

        def res_lap(i, _):
            rows = pl.ds(pl.multiple_of(at * piece + i * ROWS, ROWS), ROWS)
            res[rows, :] = total[rows, :].astype(BF16)
            return 0

        lax.fori_loop(0, piece // ROWS, res_lap, 0)

    for right in (True, False):
        for k in range(n_row - 1):
            @pl.when(x_sends(k, right))
            def _():
                for sub in order(right):
                    x_send(k, sub, right).wait_send()
        for k in range(n_col - 1):
            @pl.when(ag_sends(k, right))
            def _():
                for h in range(halves):
                    ag_send(k, h, right).wait_send()
        for step in range(n_col - 1):
            shard, valid = rs_shard(step, right)

            @pl.when(valid)
            def _():
                for ch in range(chunks):
                    rs_send(shard, ch, right).wait_send()
    for k in range(1, n_row):
        sq_copy(k).wait_send()
        pr_copy(k).wait_send()
    for to in range(n_sec - 1):
        @pl.when(me_s > to)
        def _():
            for at in range(parts):
                term_copy(to, at).wait_send()
    query_out.wait()
    normed_out.wait()


def body(mid, query_grad, top_grad, w_query, gain):
    n_sec, n_row, n_col = (lax.axis_size(a) for a in ("section", "row", "col"))
    tokens, width = mid.shape[1:]
    rows, depth = query_grad.shape[1:]
    subs = rows // tokens
    chunks, halves, parts = 4, 2, 3
    fc = width // chunks
    vmem = pl.BlockSpec(memory_space=pltpu.VMEM)
    hbm = pl.BlockSpec(memory_space=pl.ANY)
    dma = pltpu.SemaphoreType.DMA
    residual, normed, query = pl.pallas_call(
        functools.partial(kernel, n_sec, n_row, n_col, chunks, halves, parts),
        out_shape=(
            jax.ShapeDtypeStruct((tokens, width), BF16),
            jax.ShapeDtypeStruct((n_col, tokens, width), BF16),
            jax.ShapeDtypeStruct((n_col, tokens, depth), BF16),
        ),
        in_specs=[vmem, vmem, vmem, vmem, hbm],
        out_specs=(vmem, hbm, hbm),
        scratch_shapes=[
            pltpu.VMEM((width, depth), BF16),
            pltpu.VMEM((n_col, tokens, width), BF16),
            pltpu.VMEM((n_col, tokens, depth), BF16),
            pltpu.VMEM((n_col, chunks, tokens, fc), BF16),
            pltpu.VMEM((n_col, chunks, tokens, fc), BF16),
            pltpu.VMEM((n_col, chunks, tokens, fc), BF16),
            pltpu.VMEM((n_col, tokens, LANES), F32),
            pltpu.VMEM((n_row, n_col, tokens, LANES), F32),
            pltpu.VMEM((tokens, LANES), F32),
            pltpu.VMEM((n_row, tokens, LANES), F32),
            pltpu.VMEM((tokens, width), F32),
            pltpu.VMEM((tokens, width), BF16),
            pltpu.VMEM((n_sec, tokens, width), BF16),
            pltpu.VMEM((tokens, width), F32),
            pltpu.VMEM((n_col, tokens, width), BF16),
            pltpu.VMEM((n_col, tokens, LANES), F32),
            dma((chunks,)),
            dma((n_col,)), dma((n_col,)), dma((n_col,)),
            dma((n_col, halves)), dma((n_col, halves)), dma((n_col, halves)),
            dma((n_col, chunks)), dma((n_col, chunks)),
            dma((n_col, chunks)), dma((n_col, chunks)),
            dma((n_row,)), dma((n_row,)), dma((n_row,)), dma((n_row,)),
            dma((n_sec, parts)), dma((n_sec, parts)),
            dma((2,)),
        ],
        compiler_params=pltpu.CompilerParams(
            collective_id=0, has_side_effects=True, vmem_limit_bytes=58 * 1024 * 1024
        ),
    )(mid[0], query_grad[0].reshape(subs, tokens, depth), top_grad, gain, w_query[0])
    total_rows = n_col * tokens
    contracted = lax.dot_general(
        normed.reshape(total_rows, width),
        query.reshape(total_rows, depth),
        (((0,), (0,)), ((), ())),
        preferred_element_type=F32,
    )
    weight_grad = (contracted * total_rows ** (-0.5)).astype(BF16)[None]
    return (weight_grad, residual[None])


def solution(mesh):
    return jax.shard_map(
        body,
        mesh=mesh,
        in_specs=(
            P("section", ("groups", "col"), "row"),
            P("section", ("groups", "row"), "col"),
            P(("groups", "col"), "row"),
            P("section", "row", "col"),
            P("section", "row"),
        ),
        out_specs=(P(("groups", "section"), "row", "col"), P("section", ("groups", "col"), "row")),
        check_vma=False,
    )
```

time: 223 us -> 97.7 us (0.44)
  waiting for transfers between devices: 167 us -> 0 us
  Pallas kernels: 0 us -> 81.4 us
  between operations: 13.8 us -> 0.65 us
  matrix products: 26.3 us -> 14.5 us
  other arithmetic: 9.93 us -> 0 us
  blocking collectives: 4.94 us -> 0 us
    all_gather x3 -> x0, waiting for transfers between devices: 106 us -> none  [the longest x1 64.8 us: body(): lax.all_gather(normed, 'col', axis=0, tiled=True)]
    pallas_call x0 -> x1, Pallas kernels: none -> 81.4 us  [body(): pl.pallas_call(functools.partial(kernel, n_sec, n_row, n_col, chunks, hal...]
    reduce_scatter x1 -> x0, waiting for transfers between devices: 60.4 us -> none  [body(): lax.psum_scatter(lax.dot_general(block, weights, (((1,), (1,)), ((), ()))...]
    dot_general x2 -> x1, matrix products: 26.3 us -> 14.5 us  [body(): lax.dot_general(normed.reshape(total_rows, width), query.reshape(total_ro...]
    psum x1 -> x0, blocking collectives: 4.94 us -> none  [body(): lax.psum((jnp.sum(x_float * x_float, axis=1), products), 'row')]
    select_n x2 -> x0, other arithmetic: 3.96 us -> none  [lap(): return jnp.where(reached, new, before)]
    broadcast_in_dim x1 -> x0, other arithmetic: 3 us -> none  [body(): (top_grad.astype(jnp.float32) + later + own_term).astype(jnp.bfloat16)[None]]
  transfers between devices with their start and end apart: 4 -> 0, of which waited for: 4 -> 0; matrix products, arithmetic and copies ran while one was open for 0% -> 0% of each run, Pallas kernels for 0% -> 0%
where the time goes in v1:
time: 97.7 us; the launch traced here: 97.4 us
  Pallas kernels  81.4 us (83%)
  matrix products  14.5 us (15%)
    pallas_call x1, Pallas kernels, body(): pl.pallas_call(functools.partial(kernel, n_sec, n_row, n_col, chunks, hal...  81.4 us
    dot_general x1, matrix products, body(): lax.dot_general(normed.reshape(total_rows, width), query.reshape(total_ro...  14.5 us

profile of v1, /device:TPU:0, one launch (start us, length us, event | category | flops | bytes accessed | tf_op | source)
XLA Modules:
  0.0 97.4 jit_solution(3346909902523516301)
XLA Ops:
  0.6 81.4 %shard_map.68 = (bf16[96,4096]{1,0:T(8,128)(2,1)}, bf16[4,96,4096]{2,1,0:T(8,128)(2,1)}, bf16[4,96,2048]{2,1,0:T(8,128)(2,1)}) custom-call(bf16[96,4096]{1,0:T(8,128)(2,1)} %bitcast.15, bf16[2,96,2048]{2,1,0:T(8,128)(2,1)} %bitcast.16, bf16[96,4096]{1,0:T(8,128)(2,1)} %top.1, f32[1,4096]{1,0:T(1,128)} %gain.1, bf16[4096,2048]{1,0:T(8,128)(2,1)} %bitcast.14), custom_call_target="tpu_custom_call" | custom-call | tf_op jit(solution)/shard_map/pallas_call | solution.py:398
  82.0 0.0 copy-start
  82.0 14.5 %fusion.1 = bf16[1,4096,2048]{2,1,0:T(8,128)(2,1)} fusion(bf16[4,96,4096]{2,1,0:T(8,128)(2,1)} %get-tuple-element.5, bf16[4,96,2048]{2,1,0:T(8,128)(2,1)} %get-tuple-element.6), kind=kOutput, calls=%fused_computation.2 | convolution fusion | flops 6459228160 | bytes 21495808 | tf_op jit(solution)/shard_map/dot_general | solution.py:438
  96.6 0.0 copy-done
  96.6 0.9 copy.8
Async XLA Ops:
  82.0 14.5 %copy-start = (bf16[96,4096]{1,0:T(8,128)(2,1)S(1)}, bf16[96,4096]{1,0:T(8,128)(2,1)}, u32[]{:S(2)}) copy-start(bf16[96,4096]{1,0:T(8,128)(2,1)} %get-tuple-element.7) | copy-start | bytes 2359300

commit v2 on v1

--- a/solution.py
+++ b/solution.py
@@ -37,7 +37,7 @@
     mid, query, top, gain, w_hbm,
     res, normed_hbm, query_hbm,
     w_v, mid_all, query_all, part, from_left, from_right,
-    squares, squares_in, prods, prods_in, grad, term, later, total, normed, scales,
+    squares, squares_in, prods, prods_in, grad, term, later, total, normed, turned, scales,
     w_sem, x_right, x_left, x_recv, ag_right, ag_left, ag_recv,
     rs_right, rs_left, rs_from_left, rs_from_right,
     sq_send, sq_recv, pr_send, pr_recv, term_send, term_recv, out_sem,
@@ -46,7 +46,7 @@
     tokens, width = mid.shape
     subs = query.shape[0]
     fc = width // chunks
-    tile = min(512, fc)
+    tile = min(1024, fc)
     full = width * n_row
     has_left, has_right = me_c > 0, me_c < n_col - 1
 
@@ -159,6 +159,53 @@
     def _():
         from_right[n_col - 1] = jnp.zeros(from_right.shape[1:], BF16)
 
+    def sq_copy(k, shard):
+        return push(
+            squares.at[shard], squares_in.at[me_r, shard], sq_send.at[k, shard],
+            sq_recv.at[me_r, shard], "row", lax.rem(me_r + k, n_row),
+        )
+
+    def square(shard):
+        def lap(i, _):
+            rows = pl.ds(pl.multiple_of(i * ROWS, ROWS), ROWS)
+            value = mid_all[shard, rows, :].astype(F32)
+            squares[shard, rows, :] = lane_sums(value * value)
+            return 0
+
+        lax.fori_loop(0, tokens // ROWS, lap, 0)
+        for k in range(1, n_row):
+            sq_copy(k, shard).start()
+
+    def normalize(shard):
+        for k in range(1, n_row):
+            peer = lax.rem(me_r + k, n_row)
+            got = squares_in.at[peer, shard]
+            pltpu.make_async_copy(got, got, sq_recv.at[peer, shard]).wait()
+
+        def lap(i, _):
+            rows = pl.ds(pl.multiple_of(i * ROWS, ROWS), ROWS)
+            summed = squares[shard, rows, :]
+            for k in range(1, n_row):
+                summed = summed + squares_in[lax.rem(me_r + k, n_row), shard, rows, :]
+            inverse = lax.rsqrt(jnp.sum(summed, axis=1, keepdims=True) / full + EPSILON)
+            scales[shard, rows, :] = jnp.broadcast_to(inverse, (ROWS, LANES))
+            value = mid_all[shard, rows, :].astype(F32)
+            at = pl.ds(pl.multiple_of(shard * tokens + i * ROWS, ROWS), ROWS)
+            normed[at, :] = (value * inverse * gain[...]).astype(BF16)
+            return 0
+
+        lax.fori_loop(0, tokens // ROWS, lap, 0)
+
+    def normalize_step(k):
+        pl.when(me_c - k >= 0)(lambda: normalize(me_c - k))
+        pl.when(me_c + k < n_col)(lambda: normalize(me_c + k))
+
+    def square_step(k):
+        pl.when(me_c - k >= 0)(lambda: square(me_c - k))
+        pl.when(me_c + k < n_col)(lambda: square(me_c + k))
+
+    square(me_c)
+
     def x_step(k, at):
         for right in (True, False):
             piece = me_r - k if right else me_r + k
@@ -194,63 +241,63 @@
             got, got, (rs_from_left if right else rs_from_right).at[shard, ch]
         ).wait()
 
+    def rs_first(step):
+        for right in (True, False):
+            shard, valid = rs_shard(step, right)
+            before = shard + 1 if right else shard - 1
+
+            @pl.when(valid & jnp.logical_not(has_left if right else has_right))
+            def _():
+                for ch in range(chunks):
+                    if step:
+                        rs_send(before, ch, right).wait_send()
+                    rs_send(shard, ch, right).start()
+
     def rs_step(step):
         for ch in range(chunks):
             for right in (True, False):
                 shard, valid = rs_shard(step, right)
 
-                @pl.when(valid)
+                @pl.when(valid & (has_left if right else has_right))
                 def _():
-                    @pl.when(has_left if right else has_right)
-                    def _():
-                        rs_wait(shard, ch, right)
-                        came = from_left if right else from_right
-
-                        def lap(i, _):
-                            rows = pl.ds(pl.multiple_of(i * ROWS, ROWS), ROWS)
-                            part[shard, ch, rows, :] = (
-                                part[shard, ch, rows, :].astype(F32)
-                                + came[shard, ch, rows, :].astype(F32)
-                            ).astype(BF16)
-                            return 0
-
-                        lax.fori_loop(0, tokens // ROWS, lap, 0)
-
+                    rs_wait(shard, ch, right)
+                    came = from_left if right else from_right
+
+                    def lap(i, _):
+                        rows = pl.ds(pl.multiple_of(i * ROWS, ROWS), ROWS)
+                        part[shard, ch, rows, :] = (
+                            part[shard, ch, rows, :].astype(F32)
+                            + came[shard, ch, rows, :].astype(F32)
+                        ).astype(BF16)
+                        return 0
+
+                    lax.fori_loop(0, tokens // ROWS, lap, 0)
                     rs_send(shard, ch, right).start()
 
     steps = [(k, at) for k in range(1, n_row) for at in range(subs)]
     for k, at in steps[:-1]:
         x_step(k, at)
     if subs > 1:
-        rs_step(0)
+        rs_first(0)
     if n_col > 1:
         ag_step(1)
     for k, at in steps[-1:]:
         x_step(k, at)
     if subs == 1:
-        rs_step(0)
+        rs_first(0)
     query_out = pltpu.make_async_copy(query_all, query_hbm, out_sem.at[0])
     query_out.start()
+    if n_col > 1:
+        square_step(1)
+    normalize(me_c)
     for step in range(1, n_col - 1):
+        rs_first(step)
         ag_step(step + 1)
-        if step == n_col - 2:
-            break
         rs_step(step)
-
-    def square_lap(i, _):
-        shard, at = i // (tokens // ROWS), i % (tokens // ROWS)
-        rows = pl.ds(pl.multiple_of(at * ROWS, ROWS), ROWS)
-        value = mid_all[shard, rows, :].astype(F32)
-        squares[shard, rows, :] = lane_sums(value * value)
-        return 0
-
-    lax.fori_loop(0, n_col * (tokens // ROWS), square_lap, 0)
-
-    def sq_copy(k):
-        return push(
-            squares, squares_in.at[me_r], sq_send.at[k], sq_recv.at[me_r],
-            "row", lax.rem(me_r + k, n_row),
-        )
+        square_step(step + 1)
+        normalize_step(step)
+    if n_col > 1:
+        normalize_step(n_col - 1)
 
     def pr_copy(k):
         return push(
@@ -264,26 +311,13 @@
             got = ref.at[peer]
             pltpu.make_async_copy(got, got, sem.at[peer]).wait()
 
-    for k in range(1, n_row):
-        sq_copy(k).start()
-    if n_col > 2:
-        rs_step(n_col - 2)
-    await_from(squares_in, sq_recv)
-
-    def normed_lap(i, _):
-        shard, at = i // (tokens // ROWS), i % (tokens // ROWS)
-        rows = pl.ds(pl.multiple_of(at * ROWS, ROWS), ROWS)
-        summed = squares[shard, rows, :]
-        for k in range(1, n_row):
-            summed = summed + squares_in[lax.rem(me_r + k, n_row), shard, rows, :]
-        inverse = lax.rsqrt(jnp.sum(summed, axis=1, keepdims=True) / full + EPSILON)
-        scales[shard, rows, :] = jnp.broadcast_to(inverse, (ROWS, LANES))
-        value = mid_all[shard, rows, :].astype(F32)
-        normed[shard, rows, :] = (value * inverse * gain[...]).astype(BF16)
+    def turn_lap(i, _):
+        cols = pl.ds(pl.multiple_of(i * LANES, LANES), LANES)
+        turned[cols, :] = normed[:, cols].T
         return 0
 
-    lax.fori_loop(0, n_col * (tokens // ROWS), normed_lap, 0)
-    normed_out = pltpu.make_async_copy(normed, normed_hbm, out_sem.at[1])
+    lax.fori_loop(0, width // LANES, turn_lap, 0)
+    normed_out = pltpu.make_async_copy(turned, normed_hbm, out_sem.at[1])
     normed_out.start()
 
     prods[...] = jnp.zeros(prods.shape, F32)
@@ -369,12 +403,17 @@
         for step in range(n_col - 1):
             shard, valid = rs_shard(step, right)
 
+            first = jnp.logical_not(has_left if right else has_right)
+            if step < n_col - 2:
+                valid = valid & jnp.logical_not(first)
+
             @pl.when(valid)
             def _():
                 for ch in range(chunks):
                     rs_send(shard, ch, right).wait_send()
     for k in range(1, n_row):
-        sq_copy(k).wait_send()
+        for shard in range(n_col):
+            sq_copy(k, shard).wait_send()
         pr_copy(k).wait_send()
     for to in range(n_sec - 1):
         @pl.when(me_s > to)
@@ -383,6 +422,12 @@
                 term_copy(to, at).wait_send()
     query_out.wait()
     normed_out.wait()
+
+
+def weight_kernel(scale, left, right, residual, out, residual_out):
+    value = jnp.dot(left[...], right[...], preferred_element_type=F32)
+    out[...] = (value * scale).astype(BF16)
+    residual_out[...] = residual[...]
 
 
 def body(mid, query_grad, top_grad, w_query, gain):
@@ -399,7 +444,7 @@
         functools.partial(kernel, n_sec, n_row, n_col, chunks, halves, parts),
         out_shape=(
             jax.ShapeDtypeStruct((tokens, width), BF16),
-            jax.ShapeDtypeStruct((n_col, tokens, width), BF16),
+            jax.ShapeDtypeStruct((width, n_col * tokens), BF16),
             jax.ShapeDtypeStruct((n_col, tokens, depth), BF16),
         ),
         in_specs=[vmem, vmem, vmem, vmem, hbm],
@@ -419,14 +464,15 @@
             pltpu.VMEM((tokens, width), BF16),
             pltpu.VMEM((n_sec, tokens, width), BF16),
             pltpu.VMEM((tokens, width), F32),
-            pltpu.VMEM((n_col, tokens, width), BF16),
+            pltpu.VMEM((n_col * tokens, width), BF16),
+            pltpu.VMEM((width, n_col * tokens), BF16),
             pltpu.VMEM((n_col, tokens, LANES), F32),
             dma((chunks,)),
             dma((n_col,)), dma((n_col,)), dma((n_col,)),
             dma((n_col, halves)), dma((n_col, halves)), dma((n_col, halves)),
             dma((n_col, chunks)), dma((n_col, chunks)),
             dma((n_col, chunks)), dma((n_col, chunks)),
-            dma((n_row,)), dma((n_row,)), dma((n_row,)), dma((n_row,)),
+            dma((n_row, n_col)), dma((n_row, n_col)), dma((n_row,)), dma((n_row,)),
             dma((n_sec, parts)), dma((n_sec, parts)),
             dma((2,)),
         ],
@@ -435,14 +481,26 @@
         ),
     )(mid[0], query_grad[0].reshape(subs, tokens, depth), top_grad, gain, w_query[0])
     total_rows = n_col * tokens
-    contracted = lax.dot_general(
-        normed.reshape(total_rows, width),
-        query.reshape(total_rows, depth),
-        (((0,), (0,)), ((), ())),
-        preferred_element_type=F32,
-    )
-    weight_grad = (contracted * total_rows ** (-0.5)).astype(BF16)[None]
-    return (weight_grad, residual[None])
+    tall = min(512, width)
+    weight_grad, residual = pl.pallas_call(
+        functools.partial(weight_kernel, total_rows ** (-0.5)),
+        grid=(width // tall,),
+        out_shape=(
+            jax.ShapeDtypeStruct((width, depth), BF16),
+            jax.ShapeDtypeStruct((tokens, width), BF16),
+        ),
+        in_specs=[
+            pl.BlockSpec((tall, total_rows), lambda i: (i, 0)),
+            pl.BlockSpec((total_rows, depth), lambda i: (0, 0)),
+            pl.BlockSpec((tokens, tall), lambda i: (0, i)),
+        ],
+        out_specs=(
+            pl.BlockSpec((tall, depth), lambda i: (i, 0)),
+            pl.BlockSpec((tokens, tall), lambda i: (0, i)),
+        ),
+        compiler_params=pltpu.CompilerParams(vmem_limit_bytes=60 * 1024 * 1024),
+    )(normed, query.reshape(total_rows, depth), residual)
+    return (weight_grad[None], residual[None])
 
 
 def solution(mesh):

time: 97.7 us -> 96.2 us (0.985)
  matrix products: 14.5 us -> 0 us
  Pallas kernels: 81.4 us -> 95.2 us
    dot_general x1 -> x0, matrix products: 14.5 us -> none  [body(): lax.dot_general(normed.reshape(total_rows, width), query.reshape(total_ro...]
    pallas_call x0 -> x1, Pallas kernels: none -> 13.7 us  [body(): pl.pallas_call(functools.partial(weight_kernel, total_rows ** (-0.5)), gr...]
where the time goes in v2:
time: 96.2 us; the launch traced here: 95.8 us
  Pallas kernels  95.2 us (99%)
    pallas_call x1, Pallas kernels, body(): pl.pallas_call(functools.partial(kernel, n_sec, n_row, n_col, chunks, hal...  81.5 us
    pallas_call x1, Pallas kernels, body(): pl.pallas_call(functools.partial(weight_kernel, total_rows ** (-0.5)), gr...  13.7 us

profile of v2, /device:TPU:0, one launch (start us, length us, event | category | flops | bytes accessed | tf_op | source)
XLA Modules:
  0.0 95.8 jit_solution(3377308716161297725)
XLA Ops:
  0.6 81.5 %shard_map.68 = (bf16[96,4096]{1,0:T(8,128)(2,1)}, bf16[4096,384]{1,0:T(8,128)(2,1)}, bf16[4,96,2048]{2,1,0:T(8,128)(2,1)}) custom-call(bf16[96,4096]{1,0:T(8,128)(2,1)} %bitcast.8, bf16[2,96,2048]{2,1,0:T(8,128)(2,1)} %bitcast.9, bf16[96,4096]{1,0:T(8,128)(2,1)} %top.1, f32[1,4096]{1,0:T(1,128)} %gain.1, bf16[4096,2048]{1,0:T(8,128)(2,1)} %bitcast.6), custom_call_target="tpu_custom_call" | custom-call | tf_op jit(solution)/shard_map/pallas_call | solution.py:443
  82.1 13.7 %shard_map.69 = (bf16[4096,2048]{1,0:T(8,128)(2,1)}, bf16[96,4096]{1,0:T(8,128)(2,1)}) custom-call(bf16[4096,384]{1,0:T(8,128)(2,1)} %get-tuple-element.7.left, bf16[384,2048]{1,0:T(8,128)(2,1)} %bitcast.7, bf16[96,4096]{1,0:T(8,128)(2,1)} %get-tuple-element.9.residual), custom_call_target="tpu_custom_call" | custom-call | tf_op jit(solution)/shard_map/pallas_call | solution.py:485
